TPU v7x, 32 devices: a whole 2x2x4 slice. The times are simulated.
32 devices in a mesh: parts: 2 (over x), dp: 4 (over y, core), shard: 4 (over z).
Axes of the slice: x: 2, y: 2, z: 4, core: 2. Of those that a mesh axis runs over, the one named last changes fastest.
Arguments:
- projected: bfloat16 [7680, 7680], P(('parts', 'dp', 'shard')), parts along dimension 0, may hold values from -4 to 4
- residual: bfloat16 [7680, 2560], P(('parts', 'dp', 'shard')), parts along dimension 0, may hold values from -6 to 6
- out_weight: bfloat16 [2560, 2560], P(None, 'shard'), may hold values from -0.125 to 0.125
- probe_weight: bfloat16 [2, 2560, 8], replicated, may hold values from -0.125 to 0.125
- labels: int32 [7680], P(('parts', 'dp', 'shard')), parts along dimension 0, may hold values from 0 to 7
- lengths: int32 [32, 9], P(('parts', 'dp', 'shard')), parts along dimension 0, may hold values from 12 to 48, as said below
- destination: int32 [32, 9], P(('parts', 'dp', 'shard')), parts along dimension 0, may hold values from 0 to 3, as said below
Outputs:
- hidden_rows: bfloat16 [18432, 2560], P(('parts', 'dp', 'shard')), parts along dimension 0
- probe_grad: float32 [4, 2560, 8], P('parts'), parts along dimension 0
There are 2 independent parts, one for each index of `parts`. A program takes and returns all parts, laid end to end along the dimension named above; an argument that names none is the same for every part. Nothing has to cross between parts.
Inputs may be any that keep to these rules, and one draw needn't show every extreme that they name: Each row of lengths sums to 240 and holds exactly one protein of length 48. `destination`: A loader assigns at most 3 proteins to any one dp index; in every shard column one dp index is assigned exactly 3 proteins by every loader of that column.
All inputs are finite; a program needn't handle non-finite values.
Results may differ from a plain program's by a relative error of at most 0.0031.
Values may be sent and summed in bfloat16 or wider, within the bound.
No kernel may reach another device: no remote copies, remote signals or barrier semaphores. Data moves between devices by JAX's collectives and lax.ppermute only.
A program may use at most 128 MiB of HBM per device.

v0:
```python
import jax
import jax.numpy as jnp
from jax import lax
from jax.sharding import PartitionSpec as P

HS = 128
CLASSES = 8
LMAX = 48
TOK_DEV = 240


def attend(blocks, block_lengths):
    block_count = blocks.shape[0]
    span_rows = blocks.shape[1]
    head_width = blocks.shape[2] // 3
    head_count = head_width // HS
    queries = blocks[:, :, :head_width].reshape(block_count, span_rows, head_count, HS)
    key_rows = blocks[:, :, head_width : 2 * head_width].reshape(
        block_count, span_rows, head_count, HS
    )
    value_rows = blocks[:, :, 2 * head_width :].reshape(block_count, span_rows, head_count, HS)
    scores = jnp.einsum(
        "plhs,pmhs->phlm", queries, key_rows, preferred_element_type=jnp.float32
    ) * HS ** (-0.5)
    keep_mask = (jnp.arange(span_rows, dtype=jnp.int32)[None, :] < block_lengths[:, None]).astype(
        jnp.float32
    )
    weights = jnp.exp(scores) * keep_mask[:, None, None, :]
    denominator = (
        jnp.sum(weights, axis=-1, keepdims=True)
        + (block_lengths == 0).astype(jnp.float32)[:, None, None, None]
    )
    weight_low = (weights / denominator).astype(jnp.bfloat16)
    attended = jnp.einsum(
        "phlm,pmhs->plhs", weight_low, value_rows, preferred_element_type=jnp.float32
    )
    return attended.reshape(block_count * span_rows, head_width).astype(jnp.bfloat16)


def project(attended, out_weight):
    return jnp.dot(
        attended,
        lax.all_gather(out_weight, "shard", axis=1, tiled=True),
        preferred_element_type=jnp.float32,
    )


def probe_terms(represent_x, represent_h, label_rows, keep_mask, probe_weight):
    one_hot = (label_rows[:, None] == jnp.arange(CLASSES, dtype=jnp.int32)[None, :]).astype(
        jnp.float32
    )
    collected = []
    for which, represent in enumerate((represent_x, represent_h)):
        logits = jnp.dot(represent, probe_weight[which], preferred_element_type=jnp.float32)
        exponent = jnp.exp(logits)
        likelihood = exponent / jnp.sum(exponent, axis=1, keepdims=True)
        mismatch = ((likelihood - one_hot) * keep_mask[:, None] / TOK_DEV).astype(jnp.bfloat16)
        collected.append(
            lax.dot_general(
                represent, mismatch, (((0,), (0,)), ((), ())), preferred_element_type=jnp.float32
            )
        )
    return jnp.stack(collected)


def per_device(projected, residual, out_weight, probe_weight, labels, lengths, destination):
    group_size = lax.axis_size("dp")
    prot_count = lengths.shape[1]
    slot_count = -(-prot_count // group_size)
    tok_count = projected.shape[0]
    lens_own = lengths[0]
    dest_own = destination[0]
    starts = jnp.cumsum(lens_own) - lens_own
    offsets = jnp.arange(LMAX, dtype=jnp.int32)
    positions = jnp.arange(prot_count, dtype=jnp.int32)
    same_dest = dest_own[:, None] == dest_own[None, :]
    earlier = positions[:, None] > positions[None, :]
    slot_rank = jnp.sum((same_dest & earlier).astype(jnp.int32), axis=1)
    slot_match = (
        dest_own[None, None, :] == jnp.arange(group_size, dtype=jnp.int32)[:, None, None]
    ) & (slot_rank[None, None, :] == jnp.arange(slot_count, dtype=jnp.int32)[None, :, None])
    match_int = slot_match.astype(jnp.int32)
    slot_start = jnp.sum(match_int * starts, axis=2)
    slot_len = jnp.sum(match_int * lens_own, axis=2)
    block_count = group_size * slot_count
    row_index = jnp.minimum(slot_start[:, :, None] + offsets, tok_count - 1).reshape(
        group_size, slot_count * LMAX
    )
    live_rows = (offsets[None, None, :] < slot_len[:, :, None]).reshape(
        group_size, slot_count * LMAX
    )
    rows_send = jnp.where(live_rows[:, :, None], jnp.take(projected, row_index, axis=0), 0)
    resid_send = jnp.where(live_rows[:, :, None], jnp.take(residual, row_index, axis=0), 0)
    label_send = jnp.where(live_rows, jnp.take(labels, row_index), 0)
    got_labels, got_lengths = (
        lax.all_to_all(label_send, "dp", split_axis=0, concat_axis=0, tiled=True),
        lax.all_to_all(slot_len, "dp", split_axis=0, concat_axis=0, tiled=True),
    )
    got_rows, got_resid = (
        lax.all_to_all(rows_send, "dp", split_axis=0, concat_axis=0, tiled=True),
        lax.all_to_all(resid_send, "dp", split_axis=0, concat_axis=0, tiled=True),
    )
    lengths_recv = got_lengths.reshape(block_count)
    attended = attend(got_rows.reshape(block_count, LMAX, -1), lengths_recv)
    keep_mask = (offsets[None, :] < lengths_recv[:, None]).astype(jnp.float32).reshape(-1)
    represent = got_resid.reshape(block_count * LMAX, -1)
    mixed_rows = project(attended, out_weight) + represent.astype(jnp.float32)
    hidden = (mixed_rows * keep_mask[:, None]).astype(jnp.bfloat16)
    grad_terms = probe_terms(represent, hidden, got_labels.reshape(-1), keep_mask, probe_weight)
    grad_sum = lax.psum(grad_terms, ("dp", "shard"))
    return (hidden, grad_sum)


def solution(mesh):
    return jax.shard_map(
        per_device,
        mesh=mesh,
        in_specs=(
            P(("parts", "dp", "shard"), None),
            P(("parts", "dp", "shard"), None),
            P(None, "shard"),
            P(),
            P(("parts", "dp", "shard")),
            P(("parts", "dp", "shard"), None),
            P(("parts", "dp", "shard"), None),
        ),
        out_specs=(P(("parts", "dp", "shard"), None), P("parts", None, None)),
        check_vma=False,
    )
```

profile of v0, /device:TPU:8, one launch (start us, length us, event | category | flops | bytes accessed | tf_op | source)
XLA Modules:
  0.0 349.7 jit_solution(5877579920904036037)
XLA Ops:
  7.2 0.7 all-gather.2.cloned.1.call-update
  9.2 3.2 all-to-all-start.1
  13.4 4.2 %gather_fusion.1 = bf16[576,2560]{1,0:T(8,128)(2,1)} fusion(bf16[240,2560]{1,0:T(8,128)(2,1)S(1)} %copy-done, s32[1024]{0:T(1024)S(1)} %pad_clamp_fusion), kind=kCustom, calls=%fused_computation.1 | custom fusion | bytes 5900544 | tf_op jit(solution)/shard_map/jit(_take)/gather | solution.py:93
  17.6 3.9 %gather_fusion.2 = s32[576]{0:T(1024)S(1)} fusion(s32[240]{0:T(256)S(1)} %copy-done.2, s32[1024]{0:T(1024)S(1)} %pad_clamp_fusion), kind=kCustom, calls=%fused_computation.2 | custom fusion | bytes 6912 | tf_op jit(solution)/shard_map/jit(_take)/gather | solution.py:94
  22.3 3.3 all-to-all-start.3
  25.5 4.2 %select_select_fusion.1 = bf16[4,144,2560]{2,1,0:T(8,128)(2,1)} fusion(bf16[4,144,2560]{2,1,0:T(8,128)(2,1)} %bitcast.61, pred[4,144]{1,0:T(4,128)(4,1)S(1)} %get-tuple-element.8, pred[4,144]{1,0:T(4,128)(4,1)S(1)} %get-tuple-element.7), kind=kLoop, calls=%fused_computation.23 | loop fusion | flops 2949120 | bytes 5899392 | tf_op jit(solution)/shard_map/jit(_where)/select_n | solution.py:93
  29.7 22.4 %gather_fusion = bf16[576,7680]{1,0:T(8,128)(2,1)} fusion(bf16[240,7680]{1,0:T(8,128)(2,1)} %param.7, s32[1024]{0:T(1024)S(1)} %pad_clamp_fusion), kind=kCustom, calls=%fused_computation | custom fusion | bytes 17697024 | tf_op jit(solution)/shard_map/jit(_take)/gather | solution.py:92
  52.1 4.6 %all-to-all-start.2 = ((bf16[4,144,2560]{2,1,0:T(8,128)(2,1)}), bf16[4,144,2560]{2,1,0:T(8,128)(2,1)}, u32[]{:S(2)}, u32[]{:S(2)}) async-start(bf16[4,144,2560]{2,1,0:T(8,128)(2,1)} %select_select_fusion.1), calls=%async_computation.2 | async-start | bytes 5898240 | tf_op jit(solution)/shard_map/all_to_all | solution.py:101
  56.8 8.1 %select_select_fusion = bf16[4,144,7680]{2,1,0:T(8,128)(2,1)} fusion(bf16[4,144,7680]{2,1,0:T(8,128)(2,1)} %bitcast.60, pred[4,144]{1,0:T(4,128)(4,1)S(1)} %get-tuple-element.8, pred[4,144]{1,0:T(4,128)(4,1)S(1)} %get-tuple-element.7), kind=kLoop, calls=%fused_computation.3 | loop fusion | flops 8847360 | bytes 17695872 | tf_op jit(solution)/shard_map/jit(_where)/select_n | solution.py:92
  64.9 26.7 %all-to-all-done.2 = bf16[4,144,2560]{2,1,0:T(8,128)(2,1)} async-done(((bf16[4,144,2560]{2,1,0:T(8,128)(2,1)}), bf16[4,144,2560]{2,1,0:T(8,128)(2,1)}, u32[]{:S(2)}, u32[]{:S(2)}) %all-to-all-start.2) | async-done | bytes 2949152 | tf_op jit(solution)/shard_map/all_to_all | solution.py:101
  91.6 5.7 %all-to-all-start = ((bf16[4,144,7680]{2,1,0:T(8,128)(2,1)}), bf16[4,144,7680]{2,1,0:T(8,128)(2,1)}, u32[]{:S(2)}, u32[]{:S(2)}) async-start(bf16[4,144,7680]{2,1,0:T(8,128)(2,1)} %select_select_fusion), calls=%async_computation | async-start | bytes 17694720 | tf_op jit(solution)/shard_map/all_to_all | solution.py:100
  99.1 2.7 fusion.43
  101.8 2.3 convolution_bitcast_fusion.1
  104.1 91.3 %all-to-all-done = bf16[4,144,7680]{2,1,0:T(8,128)(2,1)} async-done(((bf16[4,144,7680]{2,1,0:T(8,128)(2,1)}), bf16[4,144,7680]{2,1,0:T(8,128)(2,1)}, u32[]{:S(2)}, u32[]{:S(2)}) %all-to-all-start) | async-done | bytes 8847392 | tf_op jit(solution)/shard_map/all_to_all | solution.py:100
  195.4 4.0 %slice_bitcast_fusion.2 = (bf16[12,6,20,8,128]{4,3,2,1,0:T(8,128)(2,1)S(1)}, bf16[12,6,20,8,128]{4,3,2,1,0:T(8,128)(2,1)S(1)}, bf16[12,6,20,8,128]{4,3,2,1,0:T(8,128)(2,1)S(1)}) fusion(bf16[12,48,7680]{2,1,0:T(8,128)(2,1)} %bitcast.5), kind=kLoop, calls=%fused_computation.22 | loop fusion | bytes 17694720
  199.4 1.7 fusion
  201.2 2.0 convert_bitcast_fusion
  203.2 2.6 copy.30
  205.8 28.8 %all-gather.2.cloned.1.call-done = bf16[2560,2560]{1,0:T(8,128)(2,1)} async-done(((bf16[2560,640]{1,0:T(8,128)(2,1)}), bf16[2560,2560]{1,0:T(8,128)(2,1)}) %all-gather.2.cloned.1.call-update) | async-done | bytes 13107216 | tf_op jit(solution)/shard_map/all_gather | solution.py:43
  234.6 12.4 %multiply_convert_fusion = bf16[576,2560]{1,0:T(8,128)(2,1)S(1)} fusion(bf16[576,2560]{1,0:T(8,128)(2,1)} %bitcast.9, bf16[2560,2560]{1,0:T(8,128)(2,1)} %all-gather.2.cloned.1.call-done, bf16[72,8,20,128]{3,2,1,0:T(8,128)(2,1)} %bitcast.62, f32[576]{0:T(1024)S(1)} %reshape.360), kind=kOutput, calls=%fused_computation.4 | convolution fusion | flops 7555645440 | bytes 21956864 | tf_op jit(solution)/shard_map/dot_general | solution.py:41
  246.9 0.9 fusion.42
  248.5 0.7 pad_maximum_fusion
  249.2 92.0 %all-reduce.2.cloned.1.call-done = f32[2,2560,8]{1,2,0:T(8,128)} async-done(((f32[2,2560,8]{1,2,0:T(8,128)}), f32[2,2560,8]{1,2,0:T(8,128)}) %all-reduce.2.cloned.1.call-update) | async-done | bytes 163856 | tf_op jit(solution)/shard_map/psum | solution.py:110
  341.3 1.6 copy.62
  (54 shorter events, 5.5 us)
Async XLA Ops:
  7.2 6.2 %copy-start = (bf16[240,2560]{1,0:T(8,128)(2,1)S(1)}, bf16[240,2560]{1,0:T(8,128)(2,1)}, u32[]{:S(2)}) copy-start(bf16[240,2560]{1,0:T(8,128)(2,1)} %param.8) | copy-start | bytes 3686404
  7.2 0.8 copy-start.5
  7.2 0.9 copy-start.6
  7.2 227.4 %all-gather.2.cloned.1.call-start = ((), (), s32[]{:S(2)}) async-start(), calls=%async_computation.4 | async-start | bytes 16384000 | tf_op jit(solution)/shard_map/all_gather | solution.py:43
  9.2 13.1 %all-to-all-start.1 = ((s32[4,1,3]{2,1,0:T(1,128)}), s32[4,1,3]{2,1,0:T(1,128)S(1)}, u32[]{:S(2)}, u32[]{:S(2)}) async-start(s32[4,1,3]{2,1,0:T(1,128)} %copy.27), calls=%async_computation.1 | async-start | bytes 4096 | tf_op jit(solution)/shard_map/all_to_all | solution.py:97
  13.4 4.2 %copy-start.2 = (s32[240]{0:T(256)S(1)}, s32[240]{0:T(256)}, u32[]{:S(2)}) copy-start(s32[240]{0:T(256)} %param.11) | copy-start | bytes 2884
  22.3 29.9 %all-to-all-start.3 = ((s32[4,1,144]{2,1,0:T(1,128)}), s32[4,1,144]{2,1,0:T(1,128)S(1)}, u32[]{:S(2)}, u32[]{:S(2)}) async-start(s32[4,1,144]{2,1,0:T(1,128)} %copy.31), calls=%async_computation.3 | async-start | bytes 8192 | tf_op jit(solution)/shard_map/all_to_all | solution.py:96
  52.1 39.5 %all-to-all-start.2 = ((bf16[4,144,2560]{2,1,0:T(8,128)(2,1)}), bf16[4,144,2560]{2,1,0:T(8,128)(2,1)}, u32[]{:S(2)}, u32[]{:S(2)}) async-start(bf16[4,144,2560]{2,1,0:T(8,128)(2,1)} %select_select_fusion.1), calls=%async_computation.2 | async-start | bytes 5898240 | tf_op jit(solution)/shard_map/all_to_all | solution.py:101
  64.9 34.2 %copy-start.4 = (bf16[2,2560,8]{1,2,0:T(8,128)(2,1)S(1)}, bf16[2,2560,8]{1,2,0:T(8,128)(2,1)}, u32[]{:S(2)}) copy-start(bf16[2,2560,8]{1,2,0:T(8,128)(2,1)} %param.10) | copy-start | bytes 245764
  91.6 103.8 %all-to-all-start = ((bf16[4,144,7680]{2,1,0:T(8,128)(2,1)}), bf16[4,144,7680]{2,1,0:T(8,128)(2,1)}, u32[]{:S(2)}, u32[]{:S(2)}) async-start(bf16[4,144,7680]{2,1,0:T(8,128)(2,1)} %select_select_fusion), calls=%async_computation | async-start | bytes 17694720 | tf_op jit(solution)/shard_map/all_to_all | solution.py:100
  97.3 244.0 %all-reduce.2.cloned.1.call-start = ((), (), s32[]{:S(2)}) async-start(), calls=%async_computation.5 | async-start | bytes 327680 | tf_op jit(solution)/shard_map/psum | solution.py:110
  246.9 1.6 copy-start.3
  247.8 95.0 %copy-start.1 = (bf16[240,2560]{1,0:T(8,128)(2,1)S(1)}, bf16[240,2560]{1,0:T(8,128)(2,1)}, u32[]{:S(2)}) copy-start(bf16[240,2560]{1,0:T(8,128)(2,1)} %param.8) | copy-start | bytes 3686404
Sparse Core Ops, SparseCore 0:
  9.6 224.9 all-gather.1
  249.4 91.8 all-reduce.1
where the time goes:
time: 350 us
  waiting for transfers between devices  239 us (68%)
  local copies, waits for them, and re-layouts  42 us (12%)
  matrix products  22.5 us (6%)
  starting transfers between devices  17 us (5%)
  other arithmetic  14.4 us (4%)
  between operations  14.3 us (4%)
    psum x1, waiting for transfers between devices, per_device(): grad_sum = lax.psum(grad_terms, ('dp', 'shard'))  92 us
    all_to_all x1, waiting for transfers between devices, per_device(): lax.all_to_all(rows_send, 'dp', split_axis=0, concat_axis=0, tiled=True)  91.3 us
    all_gather x1, waiting for transfers between devices, project(): lax.all_gather(out_weight, 'shard', axis=1, tiled=True)  28.8 us
    all_to_all x1, waiting for transfers between devices, per_device(): lax.all_to_all(resid_send, 'dp', split_axis=0, concat_axis=0, tiled=True)  26.7 us
    gather x1, local copies, waits for them, and re-layouts, per_device(): jnp.take(projected, row_index, axis=0)  22.4 us
    dot_general x1, matrix products, project(): jnp.dot(attended, lax.all_gather(out_weight, 'shard', axis=1, tiled=True)...  12.4 us
    select_n x1, other arithmetic, per_device(): jnp.where(live_rows[:, :, None], jnp.take(projected, row_index, axis=0), 0)  8.14 us
  transfers between devices with their start and end apart: 6, of which 4 were waited for; matrix products, arithmetic and copies ran while one was open for 18% of the time, Pallas kernels for 0%

commit v1 on v0

--- a/solution.py
+++ b/solution.py
@@ -107,7 +107,8 @@
     mixed_rows = project(attended, out_weight) + represent.astype(jnp.float32)
     hidden = (mixed_rows * keep_mask[:, None]).astype(jnp.bfloat16)
     grad_terms = probe_terms(represent, hidden, got_labels.reshape(-1), keep_mask, probe_weight)
-    grad_sum = lax.psum(grad_terms, ("dp", "shard"))
+    partial = lax.psum(grad_terms, "dp")
+    grad_sum = lax.psum(partial, "shard")
     return (hidden, grad_sum)
 
 

time: 350 us -> 330 us (0.943)
  waiting for transfers between devices: 239 us -> 218 us
    psum x1 -> x2, waiting for transfers between devices: 92 us -> 70.2 us  [the longest x1 37.1 us: per_device(): grad_sum = lax.psum(partial, 'shard')]
  transfers between devices with their start and end apart: 6 -> 7, of which waited for: 4 -> 5; matrix products, arithmetic and copies ran while one was open for 18% -> 19% of each run, Pallas kernels for 0% -> 0%
where the time goes in v1:
time: 330 us; the launch traced here: 328 us
  waiting for transfers between devices  218 us (66%)
  local copies, waits for them, and re-layouts  42 us (13%)
  matrix products  22.5 us (7%)
  starting transfers between devices  17.1 us (5%)
  other arithmetic  14.4 us (4%)
  between operations  14 us (4%)
    all_to_all x1, waiting for transfers between devices, per_device(): lax.all_to_all(rows_send, 'dp', split_axis=0, concat_axis=0, tiled=True)  91.3 us
    psum x1, waiting for transfers between devices, per_device(): grad_sum = lax.psum(partial, 'shard')  37.1 us
    psum x1, waiting for transfers between devices, per_device(): partial = lax.psum(grad_terms, 'dp')  33.1 us
    all_gather x1, waiting for transfers between devices, project(): lax.all_gather(out_weight, 'shard', axis=1, tiled=True)  28.8 us
    all_to_all x1, waiting for transfers between devices, per_device(): lax.all_to_all(resid_send, 'dp', split_axis=0, concat_axis=0, tiled=True)  26.7 us
    gather x1, local copies, waits for them, and re-layouts, per_device(): jnp.take(projected, row_index, axis=0)  22.4 us
    dot_general x1, matrix products, project(): jnp.dot(attended, lax.all_gather(out_weight, 'shard', axis=1, tiled=True)...  12.4 us
    select_n x1, other arithmetic, per_device(): jnp.where(live_rows[:, :, None], jnp.take(projected, row_index, axis=0), 0)  8.14 us
  transfers between devices with their start and end apart: 7, of which 5 were waited for; matrix products, arithmetic and copies ran while one was open for 19% of the time, Pallas kernels for 0%

profile of v1, /device:TPU:8, one launch (start us, length us, event | category | flops | bytes accessed | tf_op | source)
XLA Modules:
  0.0 327.6 jit_solution(5709629040614551625)
XLA Ops:
  7.2 0.7 all-gather.2.cloned.1.call-update
  9.2 3.2 all-to-all-start.1
  13.4 4.2 %gather_fusion.1 = bf16[576,2560]{1,0:T(8,128)(2,1)} fusion(bf16[240,2560]{1,0:T(8,128)(2,1)S(1)} %copy-done, s32[1024]{0:T(1024)S(1)} %pad_clamp_fusion), kind=kCustom, calls=%fused_computation.1 | custom fusion | bytes 5900544 | tf_op jit(solution)/shard_map/jit(_take)/gather | solution.py:93
  17.6 3.9 %gather_fusion.2 = s32[576]{0:T(1024)S(1)} fusion(s32[240]{0:T(256)S(1)} %copy-done.2, s32[1024]{0:T(1024)S(1)} %pad_clamp_fusion), kind=kCustom, calls=%fused_computation.2 | custom fusion | bytes 6912 | tf_op jit(solution)/shard_map/jit(_take)/gather | solution.py:94
  22.3 3.3 all-to-all-start.3
  25.5 4.2 %select_select_fusion.1 = bf16[4,144,2560]{2,1,0:T(8,128)(2,1)} fusion(bf16[4,144,2560]{2,1,0:T(8,128)(2,1)} %bitcast.61, pred[4,144]{1,0:T(4,128)(4,1)S(1)} %get-tuple-element.8, pred[4,144]{1,0:T(4,128)(4,1)S(1)} %get-tuple-element.7), kind=kLoop, calls=%fused_computation.23 | loop fusion | flops 2949120 | bytes 5899392 | tf_op jit(solution)/shard_map/jit(_where)/select_n | solution.py:93
  29.7 22.4 %gather_fusion = bf16[576,7680]{1,0:T(8,128)(2,1)} fusion(bf16[240,7680]{1,0:T(8,128)(2,1)} %param.7, s32[1024]{0:T(1024)S(1)} %pad_clamp_fusion), kind=kCustom, calls=%fused_computation | custom fusion | bytes 17697024 | tf_op jit(solution)/shard_map/jit(_take)/gather | solution.py:92
  52.1 4.6 %all-to-all-start.2 = ((bf16[4,144,2560]{2,1,0:T(8,128)(2,1)}), bf16[4,144,2560]{2,1,0:T(8,128)(2,1)}, u32[]{:S(2)}, u32[]{:S(2)}) async-start(bf16[4,144,2560]{2,1,0:T(8,128)(2,1)} %select_select_fusion.1), calls=%async_computation.2 | async-start | bytes 5898240 | tf_op jit(solution)/shard_map/all_to_all | solution.py:101
  56.8 8.1 %select_select_fusion = bf16[4,144,7680]{2,1,0:T(8,128)(2,1)} fusion(bf16[4,144,7680]{2,1,0:T(8,128)(2,1)} %bitcast.60, pred[4,144]{1,0:T(4,128)(4,1)S(1)} %get-tuple-element.8, pred[4,144]{1,0:T(4,128)(4,1)S(1)} %get-tuple-element.7), kind=kLoop, calls=%fused_computation.3 | loop fusion | flops 8847360 | bytes 17695872 | tf_op jit(solution)/shard_map/jit(_where)/select_n | solution.py:92
  64.9 26.7 %all-to-all-done.2 = bf16[4,144,2560]{2,1,0:T(8,128)(2,1)} async-done(((bf16[4,144,2560]{2,1,0:T(8,128)(2,1)}), bf16[4,144,2560]{2,1,0:T(8,128)(2,1)}, u32[]{:S(2)}, u32[]{:S(2)}) %all-to-all-start.2) | async-done | bytes 2949152 | tf_op jit(solution)/shard_map/all_to_all | solution.py:101
  91.6 5.7 %all-to-all-start = ((bf16[4,144,7680]{2,1,0:T(8,128)(2,1)}), bf16[4,144,7680]{2,1,0:T(8,128)(2,1)}, u32[]{:S(2)}, u32[]{:S(2)}) async-start(bf16[4,144,7680]{2,1,0:T(8,128)(2,1)} %select_select_fusion), calls=%async_computation | async-start | bytes 17694720 | tf_op jit(solution)/shard_map/all_to_all | solution.py:100
  99.1 2.7 fusion.43
  101.8 2.3 convolution_bitcast_fusion.1
  104.1 91.3 %all-to-all-done = bf16[4,144,7680]{2,1,0:T(8,128)(2,1)} async-done(((bf16[4,144,7680]{2,1,0:T(8,128)(2,1)}), bf16[4,144,7680]{2,1,0:T(8,128)(2,1)}, u32[]{:S(2)}, u32[]{:S(2)}) %all-to-all-start) | async-done | bytes 8847392 | tf_op jit(solution)/shard_map/all_to_all | solution.py:100
  195.4 4.0 %slice_bitcast_fusion.2 = (bf16[12,6,20,8,128]{4,3,2,1,0:T(8,128)(2,1)S(1)}, bf16[12,6,20,8,128]{4,3,2,1,0:T(8,128)(2,1)S(1)}, bf16[12,6,20,8,128]{4,3,2,1,0:T(8,128)(2,1)S(1)}) fusion(bf16[12,48,7680]{2,1,0:T(8,128)(2,1)} %bitcast.5), kind=kLoop, calls=%fused_computation.22 | loop fusion | bytes 17694720
  199.4 1.7 fusion
  201.2 2.0 convert_bitcast_fusion
  203.2 2.6 copy.30
  205.8 28.8 %all-gather.2.cloned.1.call-done = bf16[2560,2560]{1,0:T(8,128)(2,1)} async-done(((bf16[2560,640]{1,0:T(8,128)(2,1)}), bf16[2560,2560]{1,0:T(8,128)(2,1)}) %all-gather.2.cloned.1.call-update) | async-done | bytes 13107216 | tf_op jit(solution)/shard_map/all_gather | solution.py:43
  234.6 12.4 %multiply_convert_fusion = bf16[576,2560]{1,0:T(8,128)(2,1)S(1)} fusion(bf16[576,2560]{1,0:T(8,128)(2,1)} %bitcast.9, bf16[2560,2560]{1,0:T(8,128)(2,1)} %all-gather.2.cloned.1.call-done, bf16[72,8,20,128]{3,2,1,0:T(8,128)(2,1)} %bitcast.62, f32[576]{0:T(1024)S(1)} %reshape.360), kind=kOutput, calls=%fused_computation.4 | convolution fusion | flops 7555645440 | bytes 21956864 | tf_op jit(solution)/shard_map/dot_general | solution.py:41
  246.9 0.9 fusion.42
  249.3 33.1 %all-reduce.3.cloned.1.call-done = f32[2,2560,8]{1,2,0:T(8,128)} async-done(((f32[2,2560,8]{1,2,0:T(8,128)}), f32[2,2560,8]{1,2,0:T(8,128)}) %all-reduce.3.cloned.1.call-update) | async-done | bytes 163856 | tf_op jit(solution)/shard_map/psum | solution.py:110
  282.5 37.1 %all-reduce.5.cloned.1.call-done = f32[2,2560,8]{1,2,0:T(8,128)} async-done(((f32[2,2560,8]{1,2,0:T(8,128)}), f32[2,2560,8]{1,2,0:T(8,128)}) %all-reduce.5.cloned.1.call-update) | async-done | bytes 163856 | tf_op jit(solution)/shard_map/psum | solution.py:111
  319.5 1.6 copy.63
  (57 shorter events, 6.2 us)
Async XLA Ops:
  7.2 6.2 %copy-start = (bf16[240,2560]{1,0:T(8,128)(2,1)S(1)}, bf16[240,2560]{1,0:T(8,128)(2,1)}, u32[]{:S(2)}) copy-start(bf16[240,2560]{1,0:T(8,128)(2,1)} %param.8) | copy-start | bytes 3686404
  7.2 0.8 copy-start.5
  7.2 0.9 copy-start.6
  7.2 227.4 %all-gather.2.cloned.1.call-start = ((), (), s32[]{:S(2)}) async-start(), calls=%async_computation.4 | async-start | bytes 16384000 | tf_op jit(solution)/shard_map/all_gather | solution.py:43
  9.2 13.1 %all-to-all-start.1 = ((s32[4,1,3]{2,1,0:T(1,128)}), s32[4,1,3]{2,1,0:T(1,128)S(1)}, u32[]{:S(2)}, u32[]{:S(2)}) async-start(s32[4,1,3]{2,1,0:T(1,128)} %copy.27), calls=%async_computation.1 | async-start | bytes 4096 | tf_op jit(solution)/shard_map/all_to_all | solution.py:97
  13.4 4.2 %copy-start.2 = (s32[240]{0:T(256)S(1)}, s32[240]{0:T(256)}, u32[]{:S(2)}) copy-start(s32[240]{0:T(256)} %param.11) | copy-start | bytes 2884
  22.3 29.9 %all-to-all-start.3 = ((s32[4,1,144]{2,1,0:T(1,128)}), s32[4,1,144]{2,1,0:T(1,128)S(1)}, u32[]{:S(2)}, u32[]{:S(2)}) async-start(s32[4,1,144]{2,1,0:T(1,128)} %copy.31), calls=%async_computation.3 | async-start | bytes 8192 | tf_op jit(solution)/shard_map/all_to_all | solution.py:96
  52.1 39.5 %all-to-all-start.2 = ((bf16[4,144,2560]{2,1,0:T(8,128)(2,1)}), bf16[4,144,2560]{2,1,0:T(8,128)(2,1)}, u32[]{:S(2)}, u32[]{:S(2)}) async-start(bf16[4,144,2560]{2,1,0:T(8,128)(2,1)} %select_select_fusion.1), calls=%async_computation.2 | async-start | bytes 5898240 | tf_op jit(solution)/shard_map/all_to_all | solution.py:101
  64.9 34.2 %copy-start.4 = (bf16[2,2560,8]{1,2,0:T(8,128)(2,1)S(1)}, bf16[2,2560,8]{1,2,0:T(8,128)(2,1)}, u32[]{:S(2)}) copy-start(bf16[2,2560,8]{1,2,0:T(8,128)(2,1)} %param.10) | copy-start | bytes 245764
  91.6 103.8 %all-to-all-start = ((bf16[4,144,7680]{2,1,0:T(8,128)(2,1)}), bf16[4,144,7680]{2,1,0:T(8,128)(2,1)}, u32[]{:S(2)}, u32[]{:S(2)}) async-start(bf16[4,144,7680]{2,1,0:T(8,128)(2,1)} %select_select_fusion), calls=%async_computation | async-start | bytes 17694720 | tf_op jit(solution)/shard_map/all_to_all | solution.py:100
  97.3 185.1 %all-reduce.3.cloned.1.call-start = ((), (), s32[]{:S(2)}) async-start(), calls=%async_computation.5 | async-start | bytes 327680 | tf_op jit(solution)/shard_map/psum | solution.py:110
  246.9 1.6 copy-start.3
  247.8 73.3 %copy-start.1 = (bf16[240,2560]{1,0:T(8,128)(2,1)S(1)}, bf16[240,2560]{1,0:T(8,128)(2,1)}, u32[]{:S(2)}) copy-start(bf16[240,2560]{1,0:T(8,128)(2,1)} %param.8) | copy-start | bytes 3686404
  249.2 70.3 %all-reduce.5.cloned.1.call-start = ((), (), s32[]{:S(2)}) async-start(), calls=%async_computation.6 | async-start | bytes 327680 | tf_op jit(solution)/shard_map/psum | solution.py:111
Sparse Core Ops, SparseCore 0:
  9.6 224.9 all-gather.1
  249.4 33.0 all-reduce.2
  284.8 34.7 all-reduce.4
